TPU v7x, 256 devices: a whole 4x4x8 slice. The times are simulated.
256 devices in a mesh: dp: 4 (over x_hi, core), ctx: 64 (over z, y, x_lo).
Axes of the slice: x: 4 (x_hi: 2, x_lo: 2; x = x_hi * 2 + x_lo), y: 4, z: 8, core: 2. Of those that a mesh axis runs over, the one named last changes fastest.
Arguments:
- queries: bfloat16 [4, 8192, 2560], P('dp', 'ctx'), may hold values from -6 to 6
- keys: bfloat16 [4, 8192, 512], P('dp', 'ctx'), may hold values from -6 to 6
- values: bfloat16 [4, 8192, 512], P('dp', 'ctx'), may hold values from -6 to 6
- out_grad: bfloat16 [4, 8192, 2560], P('dp', 'ctx'), may hold values from -24 to 24
- layer_input: bfloat16 [4, 8192, 5120], P('dp', 'ctx'), may hold values from -16 to 16
- doc_lens: int32 [4, 16], P('dp'), may hold values from 1 to 1024, 8192 in all within a row
Outputs:
- attn_out: bfloat16 [4, 8192, 2560], P('dp', 'ctx')
- query_grad: bfloat16 [4, 8192, 2560], P('dp', 'ctx')
- key_grad: bfloat16 [4, 8192, 512], P('dp', 'ctx')
- value_grad: bfloat16 [4, 8192, 512], P('dp', 'ctx')
- weight_grad: float32 [5120, 1024], P(('dp', 'ctx'))
Inputs may be any that keep to these rules, and one draw needn't show every extreme that they name: `doc_lens`: the documents of a micro-batch lie end to end and fill its 8192 positions; in every micro-batch the longest has exactly 1024 positions.
All inputs are finite; a program needn't handle non-finite values.
Results may differ from a plain program's by a relative error of at most 0.029.
Values may be sent and summed in bfloat16 or wider, within the bound.
No kernel may reach another device: no remote copies, remote signals or barrier semaphores. Data moves between devices by JAX's collectives and lax.ppermute only.
A program may use at most 128 MiB of HBM per device.

v0:
```python
import math
import jax
import jax.numpy as jnp
from jax import lax
from jax.sharding import Mesh
from jax.sharding import PartitionSpec as P

D = 5120
HD = 128
NEGATIVE = -1e30
CTX = ("cz", "cw")


def shifted(block, distance, n_ctx):
    route = [(i - distance, i) for i in range(n_ctx) if 0 <= i - distance < n_ctx]
    return lax.ppermute(block, CTX, route)


def doc_index(lengths_row, positions):
    bounds = jnp.cumsum(lengths_row)
    return jnp.sum((positions[:, None] >= bounds[None, :]).astype(jnp.int32), axis=1)


def make_shards(n_data, n_cz, n_cw):
    n_context = n_cz * n_cw

    def shards(queries, keys, values, out_grad, layer_input, doc_lens):
        tok_rows = queries.shape[1]
        kv_width = keys.shape[2]
        heads_kv = kv_width // HD
        group = queries.shape[2] // kv_width
        inverse = 1.0 / math.sqrt(HD)
        blocks_back = min(8, n_context // 4)
        owned = D // (n_data * n_context)
        token_rows = layer_input[0].reshape(tok_rows, n_data, n_cz, n_cw, owned)
        column_share = lax.all_to_all(token_rows, "cw", split_axis=3, concat_axis=0, tiled=True)
        column_share = column_share.reshape(tok_rows * n_cw, n_data * n_cz * owned)
        own_pair = jnp.concatenate([keys[0], values[0]], axis=1)
        earlier = [shifted(own_pair, d, n_context) for d in range(blocks_back, 0, -1)]
        window_pair = jnp.concatenate(earlier + [own_pair], axis=0)
        span = window_pair.shape[0]
        key_win = window_pair[:, :kv_width].reshape(span, heads_kv, HD)
        value_win = window_pair[:, kv_width:].reshape(span, heads_kv, HD)
        device = lax.axis_index("cz") * n_cw + lax.axis_index("cw")
        query_pos = device * tok_rows + jnp.arange(tok_rows, dtype=jnp.int32)
        key_pos = (device - blocks_back) * tok_rows + jnp.arange(span, dtype=jnp.int32)
        query_ids = doc_index(doc_lens[0], query_pos)
        key_ids = doc_index(doc_lens[0], key_pos)
        allowed = (
            (key_pos[None, :] <= query_pos[:, None])
            & (key_ids[None, :] == query_ids[:, None])
            & (key_pos[None, :] >= 0)
        )
        query_blk = queries[0].reshape(tok_rows, heads_kv, group, HD)
        grad_blk = out_grad[0].reshape(tok_rows, heads_kv, group, HD)
        scores = (
            jnp.einsum("ighd,jgd->ghij", query_blk, key_win, preferred_element_type=jnp.float32)
            * inverse
        )
        scores = jnp.where(allowed[None, None], scores, NEGATIVE)
        peak = jnp.max(scores, axis=-1, keepdims=True)
        exponent = jnp.exp(scores - peak)
        probs = exponent / jnp.sum(exponent, axis=-1, keepdims=True)
        probs_half = probs.astype(jnp.bfloat16)
        output = jnp.einsum(
            "ghij,jgd->ighd", probs_half, value_win, preferred_element_type=jnp.float32
        )
        out_half = output.astype(jnp.bfloat16)
        delta = jnp.einsum("ighd,ighd->ghi", grad_blk, out_half, preferred_element_type=jnp.float32)
        prob_grad = jnp.einsum(
            "ighd,jgd->ghij", grad_blk, value_win, preferred_element_type=jnp.float32
        )
        score_grad = (probs * (prob_grad - delta[..., None])).astype(jnp.bfloat16)
        query_part = (
            jnp.einsum("ghij,jgd->ighd", score_grad, key_win, preferred_element_type=jnp.float32)
            * inverse
        ).astype(jnp.bfloat16)
        key_part = (
            jnp.einsum("ghij,ighd->jgd", score_grad, query_blk, preferred_element_type=jnp.float32)
            * inverse
        )
        value_part = jnp.einsum(
            "ghij,ighd->jgd", probs_half, grad_blk, preferred_element_type=jnp.float32
        )
        pair_grad = jnp.concatenate(
            [key_part.reshape(span, kv_width), value_part.reshape(span, kv_width)], axis=1
        )

        def block_back(distance):
            first_row = (blocks_back - distance) * tok_rows
            return pair_grad[first_row : first_row + tok_rows]

        total = block_back(0)
        for distance in range(1, blocks_back + 1):
            total = total + shifted(block_back(distance), -distance, n_context)
        pair_half = total.astype(jnp.bfloat16)
        grad_scale = 1.0 / math.sqrt(tok_rows * n_context * n_data)
        group_grad = lax.all_gather(pair_half, "cw", axis=0, tiled=True)
        batch_grad = lax.dot_general(
            column_share, group_grad, (((0,), (0,)), ((), ())), preferred_element_type=jnp.float32
        )
        weight_grad = lax.psum_scatter(
            batch_grad * grad_scale, ("dp", "cz"), scatter_dimension=0, tiled=True
        )
        attn_out = out_half.reshape(tok_rows, group * kv_width)[None]
        query_grad = query_part.reshape(tok_rows, group * kv_width)[None]
        key_grad = pair_half[:, :kv_width][None]
        value_grad = pair_half[:, kv_width:][None]
        return (attn_out, query_grad, key_grad, value_grad, weight_grad)

    return shards


def solution(mesh):
    n_data = mesh.shape["dp"]
    n_context = mesh.shape["ctx"]
    n_cw = 8 if n_context % 8 == 0 else n_context
    n_cz = n_context // n_cw
    split = Mesh(mesh.devices.reshape(n_data, n_cz, n_cw), ("dp", "cz", "cw"))
    tokens = P("dp", CTX, None)
    in_specs = (tokens, tokens, tokens, tokens, tokens, P("dp", None))
    out_specs = (tokens, tokens, tokens, tokens, P(("dp", "cz", "cw"), None))
    return jax.shard_map(
        make_shards(n_data, n_cz, n_cw),
        mesh=split,
        in_specs=in_specs,
        out_specs=out_specs,
        check_vma=False,
    )
```

profile of v0, /device:TPU:8, one launch (start us, length us, event | category | flops | bytes accessed | tf_op | source)
XLA Modules:
  0.0 592.5 jit_solution(1896691711848036301)
XLA Ops:
  7.2 1.1 copy.69
  8.3 1.0 copy.70
  9.4 3.4 collective-permute-start.7
  12.8 3.5 collective-permute-start.6
  16.3 3.7 collective-permute-start.2
  20.0 5.9 collective-permute-start.1
  25.9 4.5 collective-permute-start
  30.4 0.7 copy.71
  31.2 0.1 reduce.1
  31.3 0.1 convert_reduce_fusion.1
  31.4 0.1 convert_reduce_fusion
  31.5 1.9 and_and_fusion
  33.5 1.4 copy.76
  34.9 0.3 copy.72
  35.2 1.8 collective-permute-done
  37.0 9.2 %collective-permute-start.3 = (bf16[128,1024]{0,1:T(8,128)(2,1)S(1)}, bf16[128,1024]{0,1:T(8,128)(2,1)S(1)}, u32[]{:S(2)}, u32[]{:S(2)}) collective-permute-start(bf16[128,1024]{0,1:T(8,128)(2,1)S(1)} %pad_maximum_fusion.1), channel_id=1, source_target_pairs={{0,5},{1,6},{2,7},{3,8},{4,9},{5,10},{6,11},{7,12},{8,13},{9,14},{... | collective-permute-start | bytes 786440 | tf_op jit(solution)/shard_map/ppermute | solution.py:16
  46.2 1.0 constant_dynamic-update-slice_fusion.8
  47.2 1.6 collective-permute-start.4
  48.9 7.5 %collective-permute-start.5 = (bf16[128,1024]{0,1:T(8,128)(2,1)S(1)}, bf16[128,1024]{0,1:T(8,128)(2,1)S(1)}, u32[]{:S(2)}, u32[]{:S(2)}) collective-permute-start(bf16[128,1024]{0,1:T(8,128)(2,1)S(1)} %pad_maximum_fusion.1), channel_id=1, source_target_pairs={{0,3},{1,4},{2,5},{3,6},{4,7},{5,8},{6,9},{7,10},{8,11},{9,12},{10... | collective-permute-start | bytes 786440 | tf_op jit(solution)/shard_map/ppermute | solution.py:16
  56.5 0.1 constant_dynamic-update-slice_fusion.5
  56.6 5.8 collective-permute-done.4
  62.4 0.1 constant_dynamic-update-slice_fusion.3
  62.7 1.2 fusion.34
  64.0 6.9 %fusion.35 = (f32[4,5,128]{2,1,0:T(8,128)S(1)}, f32[4,5,128,1152]{2,3,1,0:T(8,128)}) fusion(pred[128,1152]{0,1:T(8,128)(4,1)S(1)} %copy-done.11, bf16[1152,4,128,1]{0,2,3,1:T(8,128)(2,1)S(1)} %bitcast.102, bf16[128,4,5,128]{0,3,2,1:T(8,128)(2,1)S(1)} %bitcast.105), kind=kOutput, calls=%fused_computation.79 | convolution fusion | flops 766772352 | bytes 13789184 | tf_op jit(solution)/shard_map/sub | solution.py:62
  70.9 5.9 fusion.7
  76.8 3.3 fusion.36
  80.0 2.0 copy.83
  82.1 5.2 fusion.14
  87.3 5.6 fusion.2
  92.9 3.3 fusion.8
  96.2 3.1 copy.82
  99.3 2.0 fusion.25
  101.4 1.9 collective-permute-start.8
  103.3 1.9 collective-permute-start.9
  105.2 1.5 collective-permute-start.10
  106.7 1.3 collective-permute-start.11
  108.0 1.3 collective-permute-start.12
  109.3 8.8 %collective-permute-done.8 = f32[128,1024]{1,0:T(8,128)S(1)} collective-permute-done((f32[128,1024]{1,0:T(8,128)S(1)}, f32[128,1024]{1,0:T(8,128)S(1)}, u32[]{:S(2)}, u32[]{:S(2)}) %collective-permute-start.8) | collective-permute-done | bytes 524320 | tf_op jit(solution)/shard_map/ppermute | solution.py:16
  118.0 1.3 collective-permute-start.13
  119.3 4.1 collective-permute-done.9
  123.4 1.3 collective-permute-start.15
  124.7 9.6 %collective-permute-done.10 = f32[128,1024]{1,0:T(8,128)S(1)} collective-permute-done((f32[128,1024]{1,0:T(8,128)S(1)}, f32[128,1024]{1,0:T(8,128)S(1)}, u32[]{:S(2)}, u32[]{:S(2)}) %collective-permute-start.10) | collective-permute-done | bytes 524320 | tf_op jit(solution)/shard_map/ppermute | solution.py:16
  134.3 1.3 collective-permute-start.14
  135.6 19.8 %collective-permute-done.11 = f32[128,1024]{1,0:T(8,128)S(1)} collective-permute-done((f32[128,1024]{1,0:T(8,128)S(1)}, f32[128,1024]{1,0:T(8,128)S(1)}, u32[]{:S(2)}, u32[]{:S(2)}) %collective-permute-start.11) | collective-permute-done | bytes 524320 | tf_op jit(solution)/shard_map/ppermute | solution.py:16
  155.4 43.6 %collective-permute-done.13 = f32[128,1024]{1,0:T(8,128)S(1)} collective-permute-done((f32[128,1024]{1,0:T(8,128)S(1)}, f32[128,1024]{1,0:T(8,128)S(1)}, u32[]{:S(2)}, u32[]{:S(2)}) %collective-permute-start.13) | collective-permute-done | bytes 524320 | tf_op jit(solution)/shard_map/ppermute | solution.py:16
  199.1 5.7 collective-permute-done.15
  204.7 32.7 %collective-permute-done.14 = f32[128,1024]{1,0:T(8,128)S(1)} collective-permute-done((f32[128,1024]{1,0:T(8,128)S(1)}, f32[128,1024]{1,0:T(8,128)S(1)}, u32[]{:S(2)}, u32[]{:S(2)}) %collective-permute-start.14) | collective-permute-done | bytes 524320 | tf_op jit(solution)/shard_map/ppermute | solution.py:16
  237.5 1.1 fusion.31
  238.6 1.8 copy.84
  240.4 0.3 reshape_squeeze.11
  240.7 1.5 copy.85
  242.2 28.6 %all_to_all.15 = bf16[128,4,8,8,20]{0,2,4,1,3:T(8,128)(2,1)S(1)} all-to-all(bf16[128,4,8,8,20]{0,2,4,1,3:T(8,128)(2,1)S(1)} %copy.85), channel_id=1, replica_groups=mesh['dp'=4,'cz'=8,'cw'=8] {'cw'}, dimensions={3} | all-to-all | bytes 2621440 | tf_op jit(solution)/shard_map/all_to_all | solution.py:36
  270.8 0.8 copy.86
  271.7 27.9 %all-gather.2.cloned.1.call-done = bf16[1024,1024]{1,0:T(8,128)(2,1)} async-done(((bf16[128,1024]{1,0:T(8,128)(2,1)}), bf16[1024,1024]{1,0:T(8,128)(2,1)}) %all-gather.2.cloned.1.call-update) | async-done | bytes 2097168 | tf_op jit(solution)/shard_map/all_gather | solution.py:98
  299.6 5.0 multiply_bitcast_fusion
  304.6 0.6 copy-done.12
  305.3 0.6 dynamic-slice
  306.5 3.9 fusion.11
  310.5 1.1 copy.88
  311.6 1.1 copy.87
  312.6 0.7 slice_bitcast_fusion
  313.4 270.1 %all-reduce.3.cloned.1.call-done = f32[640,1024]{0,1:T(8,128)} async-done(((f32[640,1024]{0,1:T(8,128)}), f32[640,1024]{0,1:T(8,128)}) %all-reduce.3.cloned.1.call-update) | async-done | bytes 2621456
  583.4 1.4 constant_dynamic-slice_fusion
  584.8 0.8 copy.89
  (47 shorter events, 0.6 us)
Async XLA Ops:
  7.2 27.7 %copy-start.10 = (bf16[1,128,2560]{2,1,0:T(8,128)(2,1)S(1)}, bf16[1,128,2560]{2,1,0:T(8,128)(2,1)}, u32[]{:S(2)}) copy-start(bf16[1,128,2560]{2,1,0:T(8,128)(2,1)} %param.6) | copy-start | bytes 1966084
  7.2 292.4 %all-gather.2.cloned.1.call-start = ((), (), s32[]{:S(2)}) async-start(), calls=%async_computation.1 | async-start | bytes 2359296 | tf_op jit(solution)/shard_map/all_gather | solution.py:98
  9.4 53.2 %collective-permute-start.7 = (bf16[128,1024]{0,1:T(8,128)(2,1)S(1)}, bf16[128,1024]{0,1:T(8,128)(2,1)S(1)}, u32[]{:S(2)}, u32[]{:S(2)}) collective-permute-start(bf16[128,1024]{0,1:T(8,128)(2,1)S(1)} %pad_maximum_fusion.1), channel_id=1, source_target_pairs={{0,1},{1,2},{2,3},{3,4},{4,5},{5,6},{6,7},{7,8},{8,9},{9,10},{10,1... | collective-permute-start | bytes 786440 | tf_op jit(solution)/shard_map/ppermute | solution.py:16
  12.8 49.7 %collective-permute-start.6 = (bf16[128,1024]{0,1:T(8,128)(2,1)S(1)}, bf16[128,1024]{0,1:T(8,128)(2,1)S(1)}, u32[]{:S(2)}, u32[]{:S(2)}) collective-permute-start(bf16[128,1024]{0,1:T(8,128)(2,1)S(1)} %pad_maximum_fusion.1), channel_id=1, source_target_pairs={{0,2},{1,3},{2,4},{3,5},{4,6},{5,7},{6,8},{7,9},{8,10},{9,11},{10,... | collective-permute-start | bytes 786440 | tf_op jit(solution)/shard_map/ppermute | solution.py:16
  16.3 32.7 %collective-permute-start.2 = (bf16[128,1024]{0,1:T(8,128)(2,1)S(1)}, bf16[128,1024]{0,1:T(8,128)(2,1)S(1)}, u32[]{:S(2)}, u32[]{:S(2)}) collective-permute-start(bf16[128,1024]{0,1:T(8,128)(2,1)S(1)} %pad_maximum_fusion.1), channel_id=1, source_target_pairs={{0,6},{1,7},{2,8},{3,9},{4,10},{5,11},{6,12},{7,13},{8,14},{9,15},... | collective-permute-start | bytes 786440 | tf_op jit(solution)/shard_map/ppermute | solution.py:16
  20.0 27.2 %collective-permute-start.1 = (bf16[128,1024]{0,1:T(8,128)(2,1)S(1)}, bf16[128,1024]{0,1:T(8,128)(2,1)S(1)}, u32[]{:S(2)}, u32[]{:S(2)}) collective-permute-start(bf16[128,1024]{0,1:T(8,128)(2,1)S(1)} %pad_maximum_fusion.1), channel_id=1, source_target_pairs={{0,7},{1,8},{2,9},{3,10},{4,11},{5,12},{6,13},{7,14},{8,15},{9,16}... | collective-permute-start | bytes 786440 | tf_op jit(solution)/shard_map/ppermute | solution.py:16
  25.9 11.1 %collective-permute-start = (bf16[128,1024]{0,1:T(8,128)(2,1)S(1)}, bf16[128,1024]{0,1:T(8,128)(2,1)}, u32[]{:S(2)}, u32[]{:S(2)}) collective-permute-start(bf16[128,1024]{0,1:T(8,128)(2,1)S(1)} %pad_maximum_fusion.1), channel_id=1, source_target_pairs={{0,8},{1,9},{2,10},{3,11},{4,12},{5,13},{6,14},{7,15},{8,16},{9,17... | collective-permute-start | bytes 786440 | tf_op jit(solution)/shard_map/ppermute | solution.py:16
  35.2 28.8 %copy-start.7 = (bf16[1,128,2560]{1,2,0:T(8,128)(2,1)}, bf16[1,128,2560]{1,2,0:T(8,128)(2,1)S(1)}, u32[]{:S(2)}) copy-start(bf16[1,128,2560]{1,2,0:T(8,128)(2,1)S(1)} %copy.72) | copy-start | bytes 1966084
  37.0 19.5 %collective-permute-start.3 = (bf16[128,1024]{0,1:T(8,128)(2,1)S(1)}, bf16[128,1024]{0,1:T(8,128)(2,1)S(1)}, u32[]{:S(2)}, u32[]{:S(2)}) collective-permute-start(bf16[128,1024]{0,1:T(8,128)(2,1)S(1)} %pad_maximum_fusion.1), channel_id=1, source_target_pairs={{0,5},{1,6},{2,7},{3,8},{4,9},{5,10},{6,11},{7,12},{8,13},{9,14},{... | collective-permute-start | bytes 786440 | tf_op jit(solution)/shard_map/ppermute | solution.py:16
  47.2 15.1 %collective-permute-start.4 = (bf16[128,1024]{0,1:T(8,128)(2,1)S(1)}, bf16[128,1024]{0,1:T(8,128)(2,1)S(1)}, u32[]{:S(2)}, u32[]{:S(2)}) collective-permute-start(bf16[128,1024]{0,1:T(8,128)(2,1)S(1)} %pad_maximum_fusion.1), channel_id=1, source_target_pairs={{0,4},{1,5},{2,6},{3,7},{4,8},{5,9},{6,10},{7,11},{8,12},{9,13},{1... | collective-permute-start | bytes 786440 | tf_op jit(solution)/shard_map/ppermute | solution.py:16
  48.9 13.5 %collective-permute-start.5 = (bf16[128,1024]{0,1:T(8,128)(2,1)S(1)}, bf16[128,1024]{0,1:T(8,128)(2,1)S(1)}, u32[]{:S(2)}, u32[]{:S(2)}) collective-permute-start(bf16[128,1024]{0,1:T(8,128)(2,1)S(1)} %pad_maximum_fusion.1), channel_id=1, source_target_pairs={{0,3},{1,4},{2,5},{3,6},{4,7},{5,8},{6,9},{7,10},{8,11},{9,12},{10... | collective-permute-start | bytes 786440 | tf_op jit(solution)/shard_map/ppermute | solution.py:16
  62.7 1.3 copy-start.11
  64.0 6.9 %copy-start.4 = (bf16[1152,512]{0,1:T(8,128)(2,1)}, bf16[1152,512]{0,1:T(8,128)(2,1)S(1)}, u32[]{:S(2)}) copy-start(bf16[1152,512]{0,1:T(8,128)(2,1)S(1)} %get-tuple-element.33) | copy-start | bytes 3538948
  76.8 3.3 copy-start
  82.1 5.2 copy-start.3
  87.3 5.6 copy-start.8
  92.9 3.3 copy-start.1
  99.3 138.2 %copy-start.2 = (f32[1152,512]{1,0:T(8,128)S(1)}, f32[1152,512]{1,0:T(8,128)}, u32[]{:S(2)}) copy-start(f32[1152,512]{1,0:T(8,128)} %copy.82) | copy-start | bytes 7077892
  101.4 16.7 %collective-permute-start.8 = (f32[128,1024]{1,0:T(8,128)S(1)}, f32[128,1024]{1,0:T(8,128)S(1)}, u32[]{:S(2)}, u32[]{:S(2)}) collective-permute-start(f32[128,1024]{1,0:T(8,128)S(1)} %get-tuple-element.25), channel_id=1, source_target_pairs={{1,0},{2,1},{3,2},{4,3},{5,4},{6,5},{7,6},{8,7},{9,8},{10,9},{11,1... | collective-permute-start | bytes 1572872 | tf_op jit(solution)/shard_map/ppermute | solution.py:16
  103.3 20.1 %collective-permute-start.9 = (f32[128,1024]{1,0:T(8,128)S(1)}, f32[128,1024]{1,0:T(8,128)S(1)}, u32[]{:S(2)}, u32[]{:S(2)}) collective-permute-start(f32[128,1024]{1,0:T(8,128)S(1)} %get-tuple-element.26), channel_id=1, source_target_pairs={{2,0},{3,1},{4,2},{5,3},{6,4},{7,5},{8,6},{9,7},{10,8},{11,9},{12,... | collective-permute-start | bytes 1572872 | tf_op jit(solution)/shard_map/ppermute | solution.py:16
  105.2 29.1 %collective-permute-start.10 = (f32[128,1024]{1,0:T(8,128)S(1)}, f32[128,1024]{1,0:T(8,128)S(1)}, u32[]{:S(2)}, u32[]{:S(2)}) collective-permute-start(f32[128,1024]{1,0:T(8,128)S(1)} %get-tuple-element.27), channel_id=1, source_target_pairs={{3,0},{4,1},{5,2},{6,3},{7,4},{8,5},{9,6},{10,7},{11,8},{12,9},{13... | collective-permute-start | bytes 1572872 | tf_op jit(solution)/shard_map/ppermute | solution.py:16
  106.7 48.7 %collective-permute-start.11 = (f32[128,1024]{1,0:T(8,128)S(1)}, f32[128,1024]{1,0:T(8,128)S(1)}, u32[]{:S(2)}, u32[]{:S(2)}) collective-permute-start(f32[128,1024]{1,0:T(8,128)S(1)} %get-tuple-element.28), channel_id=1, source_target_pairs={{4,0},{5,1},{6,2},{7,3},{8,4},{9,5},{10,6},{11,7},{12,8},{13,9},{1... | collective-permute-start | bytes 1572872 | tf_op jit(solution)/shard_map/ppermute | solution.py:16
  108.0 47.4 %collective-permute-start.12 = (f32[128,1024]{1,0:T(8,128)S(1)}, f32[128,1024]{1,0:T(8,128)S(1)}, u32[]{:S(2)}, u32[]{:S(2)}) collective-permute-start(f32[128,1024]{1,0:T(8,128)S(1)} %get-tuple-element.29), channel_id=1, source_target_pairs={{5,0},{6,1},{7,2},{8,3},{9,4},{10,5},{11,6},{12,7},{13,8},{14,9},{... | collective-permute-start | bytes 1572872 | tf_op jit(solution)/shard_map/ppermute | solution.py:16
  118.0 81.0 %collective-permute-start.13 = (f32[128,1024]{1,0:T(8,128)S(1)}, f32[128,1024]{1,0:T(8,128)S(1)}, u32[]{:S(2)}, u32[]{:S(2)}) collective-permute-start(f32[128,1024]{1,0:T(8,128)S(1)} %get-tuple-element.30), channel_id=1, source_target_pairs={{6,0},{7,1},{8,2},{9,3},{10,4},{11,5},{12,6},{13,7},{14,8},{15,9},... | collective-permute-start | bytes 1572872 | tf_op jit(solution)/shard_map/ppermute | solution.py:16
  123.4 81.3 %collective-permute-start.15 = (f32[128,1024]{1,0:T(8,128)S(1)}, f32[128,1024]{1,0:T(8,128)S(1)}, u32[]{:S(2)}, u32[]{:S(2)}) collective-permute-start(f32[128,1024]{1,0:T(8,128)S(1)} %get-tuple-element.31), channel_id=1, source_target_pairs={{8,0},{9,1},{10,2},{11,3},{12,4},{13,5},{14,6},{15,7},{16,8},{17,9... | collective-permute-start | bytes 1572872 | tf_op jit(solution)/shard_map/ppermute | solution.py:16
  134.3 103.2 %collective-permute-start.14 = (f32[128,1024]{1,0:T(8,128)S(1)}, f32[128,1024]{1,0:T(8,128)S(1)}, u32[]{:S(2)}, u32[]{:S(2)}) collective-permute-start(f32[128,1024]{1,0:T(8,128)S(1)} %get-tuple-element.32), channel_id=1, source_target_pairs={{7,0},{8,1},{9,2},{10,3},{11,4},{12,5},{13,6},{14,7},{15,8},{16,9}... | collective-permute-start | bytes 1572872 | tf_op jit(solution)/shard_map/ppermute | solution.py:16
  238.6 344.8 %all-reduce.3.cloned.1.call-start = ((), (), s32[]{:S(2)}) async-start(), calls=%async_computation.2 | async-start | bytes 5242880
  304.6 0.7 copy-start.12
  304.6 1.9 copy-start.5
  306.5 5.1 copy-start.6
  310.5 2.2 copy-start.9
Sparse Core Ops, SparseCore 0:
  238.7 60.8 all-gather.1
  304.7 278.6 all-reduce.2
where the time goes:
time: 593 us
  waiting for transfers between devices  430 us (73%)
  starting transfers between devices  51.1 us (9%)
  matrix products  33.1 us (6%)
  blocking collectives  28.6 us (5%)
  local copies, waits for them, and re-layouts  23.2 us (4%)
  between operations  15.1 us (3%)
  other arithmetic  11.4 us (2%)
    unnamed x3, waiting for transfers between devices  270 us
    ppermute x16, waiting for transfers between devices, shifted(): return lax.ppermute(block, CTX, route)  132 us
    ppermute x16, starting transfers between devices, shifted(): return lax.ppermute(block, CTX, route)  51.1 us
    all_to_all x1, blocking collectives, shards(): lax.all_to_all(token_rows, 'cw', split_axis=3, concat_axis=0, tiled=True)  28.6 us
    all_gather x1, waiting for transfers between devices, shards(): group_grad = lax.all_gather(pair_half, 'cw', axis=0, tiled=True)  27.9 us
    unnamed x44, local copies, waits for them, and re-layouts  12.8 us
  transfers between devices with their start and end apart: 18, of which 11 were waited for; matrix products, arithmetic and copies ran while one was open for 3% of the time, Pallas kernels for 0%

commit v1 on v0

--- a/solution.py
+++ b/solution.py
@@ -33,7 +33,12 @@
         blocks_back = min(8, n_context // 4)
         owned = D // (n_data * n_context)
         token_rows = layer_input[0].reshape(tok_rows, n_data, n_cz, n_cw, owned)
-        column_share = lax.all_to_all(token_rows, "cw", split_axis=3, concat_axis=0, tiled=True)
+        column_share = jnp.concatenate(
+            lax.all_to_all(
+                jnp.stack(jnp.split(token_rows, lax.axis_size("cw"), axis=3)), "cw", 0, 0
+            ),
+            axis=0,
+        )
         column_share = column_share.reshape(tok_rows * n_cw, n_data * n_cz * owned)
         own_pair = jnp.concatenate([keys[0], values[0]], axis=1)
         earlier = [shifted(own_pair, d, n_context) for d in range(blocks_back, 0, -1)]

time: 593 us -> 437 us (0.74)
  waiting for transfers between devices: 430 us -> 188 us
  blocking collectives: 28.6 us -> 88 us
  starting transfers between devices: 51.1 us -> 74.8 us
    unnamed x3 -> x7, waiting for transfers between devices: 270 us -> 3.89 us
    unnamed x0 -> x1, blocking collectives: none -> 88 us
    all_to_all x1 -> x0, blocking collectives: 28.6 us -> none  [shards(): lax.all_to_all(token_rows, 'cw', split_axis=3, concat_axis=0, tiled=True)]
    all_to_all x0 -> x1, waiting for transfers between devices: none -> 24.3 us  [shards(): lax.all_to_all(jnp.stack(jnp.split(token_rows, lax.axis_size('cw'), axis=...]
    unnamed x1 -> x6, starting transfers between devices: 0.04 us -> 20.2 us
    unnamed x44 -> x52, local copies, waits for them, and re-layouts: 12.8 us -> 11.7 us
  transfers between devices with their start and end apart: 18 -> 24, of which waited for: 11 -> 13; matrix products, arithmetic and copies ran while one was open for 3% -> 4% of each run, Pallas kernels for 0% -> 0%
where the time goes in v1:
time: 437 us; the launch traced here: 432 us
  waiting for transfers between devices  188 us (43%)
  blocking collectives  88 us (20%)
  starting transfers between devices  74.8 us (17%)
  matrix products  32.7 us (7%)
  local copies, waits for them, and re-layouts  21.9 us (5%)
  between operations  15.3 us (4%)
  other arithmetic  11.4 us (3%)
    ppermute x16, waiting for transfers between devices, shifted(): return lax.ppermute(block, CTX, route)  132 us
    unnamed x1, blocking collectives  88 us
    ppermute x16, starting transfers between devices, shifted(): return lax.ppermute(block, CTX, route)  51.1 us
    all_gather x1, waiting for transfers between devices, shards(): group_grad = lax.all_gather(pair_half, 'cw', axis=0, tiled=True)  27.7 us
    all_to_all x1, waiting for transfers between devices, shards(): lax.all_to_all(jnp.stack(jnp.split(token_rows, lax.axis_size('cw'), axis=...  24.3 us
    unnamed x6, starting transfers between devices  20.2 us
    unnamed x52, local copies, waits for them, and re-layouts  11.7 us
  transfers between devices with their start and end apart: 24, of which 13 were waited for; matrix products, arithmetic and copies ran while one was open for 4% of the time, Pallas kernels for 0%

profile of v1, /device:TPU:8, one launch (start us, length us, event | category | flops | bytes accessed | tf_op | source)
XLA Modules:
  0.0 431.8 jit_solution(9384315331336903333)
XLA Ops:
  7.2 1.1 copy.89
  8.3 1.0 copy.90
  9.4 3.4 collective-permute-start.7
  12.8 3.5 collective-permute-start.6
  16.3 3.7 collective-permute-start.2
  20.0 5.9 %collective-permute-start.1 = (bf16[128,1024]{0,1:T(8,128)(2,1)S(1)}, bf16[128,1024]{0,1:T(8,128)(2,1)S(1)}, u32[]{:S(2)}, u32[]{:S(2)}) collective-permute-start(bf16[128,1024]{0,1:T(8,128)(2,1)S(1)} %pad_maximum_fusion.1), channel_id=1, source_target_pairs={{0,7},{1,8},{2,9},{3,10},{4,11},{5,12},{6,13},{7,14},{8,15},{9,16}... | collective-permute-start | bytes 786440 | tf_op jit(solution)/shard_map/ppermute | solution.py:16
  25.9 4.5 %collective-permute-start = (bf16[128,1024]{0,1:T(8,128)(2,1)S(1)}, bf16[128,1024]{0,1:T(8,128)(2,1)}, u32[]{:S(2)}, u32[]{:S(2)}) collective-permute-start(bf16[128,1024]{0,1:T(8,128)(2,1)S(1)} %pad_maximum_fusion.1), channel_id=1, source_target_pairs={{0,8},{1,9},{2,10},{3,11},{4,12},{5,13},{6,14},{7,15},{8,16},{9,17... | collective-permute-start | bytes 786440 | tf_op jit(solution)/shard_map/ppermute | solution.py:16
  30.5 0.7 copy.91
  31.5 1.9 and_and_fusion
  33.5 1.4 copy.96
  35.2 1.8 collective-permute-done
  37.0 9.2 %collective-permute-start.3 = (bf16[128,1024]{0,1:T(8,128)(2,1)S(1)}, bf16[128,1024]{0,1:T(8,128)(2,1)S(1)}, u32[]{:S(2)}, u32[]{:S(2)}) collective-permute-start(bf16[128,1024]{0,1:T(8,128)(2,1)S(1)} %pad_maximum_fusion.1), channel_id=1, source_target_pairs={{0,5},{1,6},{2,7},{3,8},{4,9},{5,10},{6,11},{7,12},{8,13},{9,14},{... | collective-permute-start | bytes 786440 | tf_op jit(solution)/shard_map/ppermute | solution.py:16
  46.2 1.0 constant_dynamic-update-slice_fusion.8
  47.2 1.6 collective-permute-start.4
  48.9 7.5 %collective-permute-start.5 = (bf16[128,1024]{0,1:T(8,128)(2,1)S(1)}, bf16[128,1024]{0,1:T(8,128)(2,1)S(1)}, u32[]{:S(2)}, u32[]{:S(2)}) collective-permute-start(bf16[128,1024]{0,1:T(8,128)(2,1)S(1)} %pad_maximum_fusion.1), channel_id=1, source_target_pairs={{0,3},{1,4},{2,5},{3,6},{4,7},{5,8},{6,9},{7,10},{8,11},{9,12},{10... | collective-permute-start | bytes 786440 | tf_op jit(solution)/shard_map/ppermute | solution.py:16
  56.6 5.8 %collective-permute-done.4 = bf16[128,1024]{0,1:T(8,128)(2,1)S(1)} collective-permute-done((bf16[128,1024]{0,1:T(8,128)(2,1)S(1)}, bf16[128,1024]{0,1:T(8,128)(2,1)S(1)}, u32[]{:S(2)}, u32[]{:S(2)}) %collective-permute-start.4) | collective-permute-done | bytes 262176 | tf_op jit(solution)/shard_map/ppermute | solution.py:16
  62.7 1.2 fusion.43
  64.0 6.9 %fusion.44 = (f32[4,5,128]{2,1,0:T(8,128)S(1)}, f32[4,5,128,1152]{2,3,1,0:T(8,128)}) fusion(pred[128,1152]{0,1:T(8,128)(4,1)S(1)} %copy-done.11, bf16[1152,4,128,1]{0,2,3,1:T(8,128)(2,1)S(1)} %bitcast.140, bf16[128,4,5,128]{0,3,2,1:T(8,128)(2,1)S(1)} %bitcast.143), kind=kOutput, calls=%fused_computation.95 | convolution fusion | flops 766772352 | bytes 13789184 | tf_op jit(solution)/shard_map/sub | solution.py:67
  70.9 5.9 %fusion.8 = bf16[4,5,128,1152]{2,3,1,0:T(8,128)(2,1)S(1)} fusion(f32[4,5,128,1152]{2,3,1,0:T(8,128)} %get-tuple-element.38, f32[4,5,128]{2,1,0:T(8,128)S(1)} %get-tuple-element.37), kind=kLoop, calls=%fused_computation.27 | loop fusion | flops 5898240 | bytes 17704960 | tf_op jit(solution)/shard_map/convert_element_type | solution.py:69
  76.8 3.3 fusion.45
  80.0 2.0 copy.103
  82.1 5.2 %fusion.15 = (f32[4,5,128]{2,1,0:T(8,128)S(1)}, bf16[4,128,5,128]{3,1,2,0:T(8,128)(2,1)}) fusion(bf16[4,5,128,128]{2,3,1,0:T(8,128)(2,1)S(1)} %bitcast.136, bf16[1152,4,128,1]{0,2,3,1:T(8,128)(2,1)} %bitcast.138, bf16[4,5,128,1152]{2,3,1,0:T(8,128)(2,1)} %copy-done), kind=kOutput, calls=%fused_computation.38 | convolution fusion | flops 756610560 | bytes 8398848 | tf_op jit(solution)/shard_map/ghij,jgd->ighd/dot_general | solution.py:70
  87.3 5.6 %fusion.3 = bf16[4,5,128,1152]{2,3,1,0:T(8,128)(2,1)S(1)} fusion(bf16[1152,4,128,1]{0,2,3,1:T(8,128)(2,1)S(1)} %bitcast.139, bf16[128,4,5,128]{0,3,2,1:T(8,128)(2,1)S(1)} %bitcast.137, f32[4,5,128]{2,1,0:T(8,128)S(1)} %get-tuple-element.39, f32[4,5,128,1152]{2,3,1,0:T(8,128)} %get-tuple-element.38, f32[4,5,128]{2,1,0:T(8,128)S(1)} %get-tuple-element.37), kind=kOutput, calls=%fused_computation.3 | convolution fusion | flops 766771200 | bytes 19550208 | tf_op jit(solution)/shard_map/ighd,jgd->ghij/dot_general | solution.py:75
  92.9 3.3 fusion.9
  96.2 3.1 copy.102
  99.3 2.0 fusion.26
  101.3 1.9 collective-permute-start.8
  103.3 1.9 collective-permute-start.9
  105.2 1.5 collective-permute-start.10
  106.7 1.3 collective-permute-start.11
  108.0 1.3 collective-permute-start.12
  109.3 8.8 %collective-permute-done.8 = f32[128,1024]{1,0:T(8,128)S(1)} collective-permute-done((f32[128,1024]{1,0:T(8,128)S(1)}, f32[128,1024]{1,0:T(8,128)S(1)}, u32[]{:S(2)}, u32[]{:S(2)}) %collective-permute-start.8) | collective-permute-done | bytes 524320 | tf_op jit(solution)/shard_map/ppermute | solution.py:16
  118.0 1.3 collective-permute-start.13
  119.3 4.1 collective-permute-done.9
  123.4 1.3 collective-permute-start.15
  124.7 9.6 %collective-permute-done.10 = f32[128,1024]{1,0:T(8,128)S(1)} collective-permute-done((f32[128,1024]{1,0:T(8,128)S(1)}, f32[128,1024]{1,0:T(8,128)S(1)}, u32[]{:S(2)}, u32[]{:S(2)}) %collective-permute-start.10) | collective-permute-done | bytes 524320 | tf_op jit(solution)/shard_map/ppermute | solution.py:16
  134.3 1.3 collective-permute-start.14
  135.5 19.9 %collective-permute-done.11 = f32[128,1024]{1,0:T(8,128)S(1)} collective-permute-done((f32[128,1024]{1,0:T(8,128)S(1)}, f32[128,1024]{1,0:T(8,128)S(1)}, u32[]{:S(2)}, u32[]{:S(2)}) %collective-permute-start.11) | collective-permute-done | bytes 524320 | tf_op jit(solution)/shard_map/ppermute | solution.py:16
  155.4 43.5 %collective-permute-done.13 = f32[128,1024]{1,0:T(8,128)S(1)} collective-permute-done((f32[128,1024]{1,0:T(8,128)S(1)}, f32[128,1024]{1,0:T(8,128)S(1)}, u32[]{:S(2)}, u32[]{:S(2)}) %collective-permute-start.13) | collective-permute-done | bytes 524320 | tf_op jit(solution)/shard_map/ppermute | solution.py:16
  198.9 5.8 %collective-permute-done.15 = f32[128,1024]{1,0:T(8,128)S(1)} collective-permute-done((f32[128,1024]{1,0:T(8,128)S(1)}, f32[128,1024]{1,0:T(8,128)S(1)}, u32[]{:S(2)}, u32[]{:S(2)}) %collective-permute-start.15) | collective-permute-done | bytes 524320 | tf_op jit(solution)/shard_map/ppermute | solution.py:16
  204.7 32.7 %collective-permute-done.14 = f32[128,1024]{1,0:T(8,128)S(1)} collective-permute-done((f32[128,1024]{1,0:T(8,128)S(1)}, f32[128,1024]{1,0:T(8,128)S(1)}, u32[]{:S(2)}, u32[]{:S(2)}) %collective-permute-start.14) | collective-permute-done | bytes 524320 | tf_op jit(solution)/shard_map/ppermute | solution.py:16
  237.4 1.1 fusion.32
  238.5 1.8 copy.104
  240.9 1.3 copy.113
  242.2 3.5 all-to-all-start
  247.0 24.3 %all-to-all-done = bf16[8,128,4,8,1,20]{1,3,5,4,2,0:T(8,128)(2,1)S(1)} async-done(((bf16[8,128,4,8,1,20]{1,3,5,4,2,0:T(8,128)(2,1)}), bf16[8,128,4,8,1,20]{1,3,5,4,2,0:T(8,128)(2,1)S(1)}, u32[]{:S(2)}, u32[]{:S(2)}) %all-to-all-start) | async-done | bytes 1310752 | tf_op jit(solution)/shard_map/all_to_all | solution.py:37
  271.3 0.8 copy.114
  272.1 27.7 %all-gather.2.cloned.1.call-done = bf16[1024,1024]{1,0:T(8,128)(2,1)} async-done(((bf16[128,1024]{1,0:T(8,128)(2,1)}), bf16[1024,1024]{1,0:T(8,128)(2,1)}) %all-gather.2.cloned.1.call-update) | async-done | bytes 2097168 | tf_op jit(solution)/shard_map/all_gather | solution.py:103
  299.8 4.7 %convolution_multiply_fusion = f32[640,1024]{1,0:T(8,128)} fusion(bf16[1024,1024]{1,0:T(8,128)(2,1)} %all-gather.2.cloned.1.call-done, bf16[80,8,8,128]{3,2,1,0:T(8,128)(2,1)S(1)} %bitcast.146), kind=kOutput, calls=%fused_computation.31 | convolution fusion | flops 1342832640 | bytes 6029312 | tf_op jit(solution)/shard_map/dot_general | solution.py:104
  304.4 88.0 %fusion = f32[24,1024]{1,0:T(8,128)S(1)} fusion(f32[640,1024]{1,0:T(8,128)} %convolution_multiply_fusion), kind=kCustom, calls=%all-reduce-scatter | all-reduce-scatter fusion | flops 786433 | bytes 2720768
  392.5 1.4 collective-permute-start.21
  393.9 3.9 fusion.12
  397.8 1.1 copy.116
  398.9 1.1 copy.115
  400.0 1.3 collective-permute-start.20
  401.3 5.2 %collective-permute-start.19 = (f32[24,1024]{1,0:T(8,128)S(1)}, f32[24,1024]{1,0:T(8,128)S(1)}, u32[]{:S(2)}, u32[]{:S(2)}) collective-permute-start(f32[24,1024]{1,0:T(8,128)S(1)} %fusion), channel_id=1, source_target_pairs={{0,32},{8,40},{16,48},{24,56},{32,64},{40,72},{48,80},{56,88},{64,... | collective-permute-start | bytes 294920
  406.5 5.1 %collective-permute-start.18 = (f32[24,1024]{1,0:T(8,128)S(1)}, f32[24,1024]{1,0:T(8,128)S(1)}, u32[]{:S(2)}, u32[]{:S(2)}) collective-permute-start(f32[24,1024]{1,0:T(8,128)S(1)} %fusion), channel_id=1, source_target_pairs={{0,24},{8,32},{16,40},{24,48},{32,56},{40,64},{48,72},{56,80},{64,... | collective-permute-start | bytes 294920
  411.6 3.8 collective-permute-start.17
  415.4 3.4 collective-permute-start.16
  418.8 0.7 slice_bitcast_fusion.8
  419.5 2.6 collective-permute-done.17
  422.1 1.3 collective-permute-done.16
  423.4 0.9 concatenate.12
  424.3 0.7 constant_dynamic-slice_fusion
  (67 shorter events, 2.5 us)
Async XLA Ops:
  7.2 27.7 %copy-start.10 = (bf16[1,128,2560]{2,1,0:T(8,128)(2,1)S(1)}, bf16[1,128,2560]{2,1,0:T(8,128)(2,1)}, u32[]{:S(2)}) copy-start(bf16[1,128,2560]{2,1,0:T(8,128)(2,1)} %param.6) | copy-start | bytes 1966084
  7.2 292.6 %all-gather.2.cloned.1.call-start = ((), (), s32[]{:S(2)}) async-start(), calls=%async_computation.1 | async-start | bytes 2359296 | tf_op jit(solution)/shard_map/all_gather | solution.py:103
  9.4 53.2 %collective-permute-start.7 = (bf16[128,1024]{0,1:T(8,128)(2,1)S(1)}, bf16[128,1024]{0,1:T(8,128)(2,1)S(1)}, u32[]{:S(2)}, u32[]{:S(2)}) collective-permute-start(bf16[128,1024]{0,1:T(8,128)(2,1)S(1)} %pad_maximum_fusion.1), channel_id=1, source_target_pairs={{0,1},{1,2},{2,3},{3,4},{4,5},{5,6},{6,7},{7,8},{8,9},{9,10},{10,1... | collective-permute-start | bytes 786440 | tf_op jit(solution)/shard_map/ppermute | solution.py:16
  12.8 49.7 %collective-permute-start.6 = (bf16[128,1024]{0,1:T(8,128)(2,1)S(1)}, bf16[128,1024]{0,1:T(8,128)(2,1)S(1)}, u32[]{:S(2)}, u32[]{:S(2)}) collective-permute-start(bf16[128,1024]{0,1:T(8,128)(2,1)S(1)} %pad_maximum_fusion.1), channel_id=1, source_target_pairs={{0,2},{1,3},{2,4},{3,5},{4,6},{5,7},{6,8},{7,9},{8,10},{9,11},{10,... | collective-permute-start | bytes 786440 | tf_op jit(solution)/shard_map/ppermute | solution.py:16
  16.3 32.7 %collective-permute-start.2 = (bf16[128,1024]{0,1:T(8,128)(2,1)S(1)}, bf16[128,1024]{0,1:T(8,128)(2,1)S(1)}, u32[]{:S(2)}, u32[]{:S(2)}) collective-permute-start(bf16[128,1024]{0,1:T(8,128)(2,1)S(1)} %pad_maximum_fusion.1), channel_id=1, source_target_pairs={{0,6},{1,7},{2,8},{3,9},{4,10},{5,11},{6,12},{7,13},{8,14},{9,15},... | collective-permute-start | bytes 786440 | tf_op jit(solution)/shard_map/ppermute | solution.py:16
  20.0 27.2 %collective-permute-start.1 = (bf16[128,1024]{0,1:T(8,128)(2,1)S(1)}, bf16[128,1024]{0,1:T(8,128)(2,1)S(1)}, u32[]{:S(2)}, u32[]{:S(2)}) collective-permute-start(bf16[128,1024]{0,1:T(8,128)(2,1)S(1)} %pad_maximum_fusion.1), channel_id=1, source_target_pairs={{0,7},{1,8},{2,9},{3,10},{4,11},{5,12},{6,13},{7,14},{8,15},{9,16}... | collective-permute-start | bytes 786440 | tf_op jit(solution)/shard_map/ppermute | solution.py:16
  25.9 11.1 %collective-permute-start = (bf16[128,1024]{0,1:T(8,128)(2,1)S(1)}, bf16[128,1024]{0,1:T(8,128)(2,1)}, u32[]{:S(2)}, u32[]{:S(2)}) collective-permute-start(bf16[128,1024]{0,1:T(8,128)(2,1)S(1)} %pad_maximum_fusion.1), channel_id=1, source_target_pairs={{0,8},{1,9},{2,10},{3,11},{4,12},{5,13},{6,14},{7,15},{8,16},{9,17... | collective-permute-start | bytes 786440 | tf_op jit(solution)/shard_map/ppermute | solution.py:16
  35.2 28.8 %copy-start.7 = (bf16[1,128,2560]{1,2,0:T(8,128)(2,1)}, bf16[1,128,2560]{1,2,0:T(8,128)(2,1)S(1)}, u32[]{:S(2)}) copy-start(bf16[1,128,2560]{1,2,0:T(8,128)(2,1)S(1)} %copy.92) | copy-start | bytes 1966084
  37.0 19.5 %collective-permute-start.3 = (bf16[128,1024]{0,1:T(8,128)(2,1)S(1)}, bf16[128,1024]{0,1:T(8,128)(2,1)S(1)}, u32[]{:S(2)}, u32[]{:S(2)}) collective-permute-start(bf16[128,1024]{0,1:T(8,128)(2,1)S(1)} %pad_maximum_fusion.1), channel_id=1, source_target_pairs={{0,5},{1,6},{2,7},{3,8},{4,9},{5,10},{6,11},{7,12},{8,13},{9,14},{... | collective-permute-start | bytes 786440 | tf_op jit(solution)/shard_map/ppermute | solution.py:16
  47.2 15.1 %collective-permute-start.4 = (bf16[128,1024]{0,1:T(8,128)(2,1)S(1)}, bf16[128,1024]{0,1:T(8,128)(2,1)S(1)}, u32[]{:S(2)}, u32[]{:S(2)}) collective-permute-start(bf16[128,1024]{0,1:T(8,128)(2,1)S(1)} %pad_maximum_fusion.1), channel_id=1, source_target_pairs={{0,4},{1,5},{2,6},{3,7},{4,8},{5,9},{6,10},{7,11},{8,12},{9,13},{1... | collective-permute-start | bytes 786440 | tf_op jit(solution)/shard_map/ppermute | solution.py:16
  48.9 13.5 %collective-permute-start.5 = (bf16[128,1024]{0,1:T(8,128)(2,1)S(1)}, bf16[128,1024]{0,1:T(8,128)(2,1)S(1)}, u32[]{:S(2)}, u32[]{:S(2)}) collective-permute-start(bf16[128,1024]{0,1:T(8,128)(2,1)S(1)} %pad_maximum_fusion.1), channel_id=1, source_target_pairs={{0,3},{1,4},{2,5},{3,6},{4,7},{5,8},{6,9},{7,10},{8,11},{9,12},{10... | collective-permute-start | bytes 786440 | tf_op jit(solution)/shard_map/ppermute | solution.py:16
  62.7 1.3 copy-start.11
  64.0 6.9 %copy-start.4 = (bf16[1152,512]{0,1:T(8,128)(2,1)}, bf16[1152,512]{0,1:T(8,128)(2,1)S(1)}, u32[]{:S(2)}) copy-start(bf16[1152,512]{0,1:T(8,128)(2,1)S(1)} %get-tuple-element.33) | copy-start | bytes 3538948
  76.8 3.3 copy-start
  82.1 5.2 %copy-start.3 = (bf16[1152,512]{0,1:T(8,128)(2,1)S(1)}, bf16[1152,512]{0,1:T(8,128)(2,1)}, u32[]{:S(2)}) copy-start(bf16[1152,512]{0,1:T(8,128)(2,1)} %get-tuple-element.34) | copy-start | bytes 3538948
  87.3 5.6 %copy-start.8 = (bf16[1,128,2560]{1,2,0:T(8,128)(2,1)S(1)}, bf16[1,128,2560]{1,2,0:T(8,128)(2,1)}, u32[]{:S(2)}) copy-start(bf16[1,128,2560]{1,2,0:T(8,128)(2,1)} %copy-done.7) | copy-start | bytes 1966084
  92.9 3.3 copy-start.1
  99.3 138.1 %copy-start.2 = (f32[1152,512]{1,0:T(8,128)S(1)}, f32[1152,512]{1,0:T(8,128)}, u32[]{:S(2)}) copy-start(f32[1152,512]{1,0:T(8,128)} %copy.102) | copy-start | bytes 7077892
  101.3 16.7 %collective-permute-start.8 = (f32[128,1024]{1,0:T(8,128)S(1)}, f32[128,1024]{1,0:T(8,128)S(1)}, u32[]{:S(2)}, u32[]{:S(2)}) collective-permute-start(f32[128,1024]{1,0:T(8,128)S(1)} %get-tuple-element.25), channel_id=1, source_target_pairs={{1,0},{2,1},{3,2},{4,3},{5,4},{6,5},{7,6},{8,7},{9,8},{10,9},{11,1... | collective-permute-start | bytes 1572872 | tf_op jit(solution)/shard_map/ppermute | solution.py:16
  103.3 20.1 %collective-permute-start.9 = (f32[128,1024]{1,0:T(8,128)S(1)}, f32[128,1024]{1,0:T(8,128)S(1)}, u32[]{:S(2)}, u32[]{:S(2)}) collective-permute-start(f32[128,1024]{1,0:T(8,128)S(1)} %get-tuple-element.26), channel_id=1, source_target_pairs={{2,0},{3,1},{4,2},{5,3},{6,4},{7,5},{8,6},{9,7},{10,8},{11,9},{12,... | collective-permute-start | bytes 1572872 | tf_op jit(solution)/shard_map/ppermute | solution.py:16
  105.2 29.1 %collective-permute-start.10 = (f32[128,1024]{1,0:T(8,128)S(1)}, f32[128,1024]{1,0:T(8,128)S(1)}, u32[]{:S(2)}, u32[]{:S(2)}) collective-permute-start(f32[128,1024]{1,0:T(8,128)S(1)} %get-tuple-element.27), channel_id=1, source_target_pairs={{3,0},{4,1},{5,2},{6,3},{7,4},{8,5},{9,6},{10,7},{11,8},{12,9},{13... | collective-permute-start | bytes 1572872 | tf_op jit(solution)/shard_map/ppermute | solution.py:16
  106.7 48.7 %collective-permute-start.11 = (f32[128,1024]{1,0:T(8,128)S(1)}, f32[128,1024]{1,0:T(8,128)S(1)}, u32[]{:S(2)}, u32[]{:S(2)}) collective-permute-start(f32[128,1024]{1,0:T(8,128)S(1)} %get-tuple-element.28), channel_id=1, source_target_pairs={{4,0},{5,1},{6,2},{7,3},{8,4},{9,5},{10,6},{11,7},{12,8},{13,9},{1... | collective-permute-start | bytes 1572872 | tf_op jit(solution)/shard_map/ppermute | solution.py:16
  108.0 47.4 %collective-permute-start.12 = (f32[128,1024]{1,0:T(8,128)S(1)}, f32[128,1024]{1,0:T(8,128)S(1)}, u32[]{:S(2)}, u32[]{:S(2)}) collective-permute-start(f32[128,1024]{1,0:T(8,128)S(1)} %get-tuple-element.29), channel_id=1, source_target_pairs={{5,0},{6,1},{7,2},{8,3},{9,4},{10,5},{11,6},{12,7},{13,8},{14,9},{... | collective-permute-start | bytes 1572872 | tf_op jit(solution)/shard_map/ppermute | solution.py:16
  118.0 80.9 %collective-permute-start.13 = (f32[128,1024]{1,0:T(8,128)S(1)}, f32[128,1024]{1,0:T(8,128)S(1)}, u32[]{:S(2)}, u32[]{:S(2)}) collective-permute-start(f32[128,1024]{1,0:T(8,128)S(1)} %get-tuple-element.30), channel_id=1, source_target_pairs={{6,0},{7,1},{8,2},{9,3},{10,4},{11,5},{12,6},{13,7},{14,8},{15,9},... | collective-permute-start | bytes 1572872 | tf_op jit(solution)/shard_map/ppermute | solution.py:16
  123.4 81.3 %collective-permute-start.15 = (f32[128,1024]{1,0:T(8,128)S(1)}, f32[128,1024]{1,0:T(8,128)S(1)}, u32[]{:S(2)}, u32[]{:S(2)}) collective-permute-start(f32[128,1024]{1,0:T(8,128)S(1)} %get-tuple-element.31), channel_id=1, source_target_pairs={{8,0},{9,1},{10,2},{11,3},{12,4},{13,5},{14,6},{15,7},{16,8},{17,9... | collective-permute-start | bytes 1572872 | tf_op jit(solution)/shard_map/ppermute | solution.py:16
  134.3 103.1 %collective-permute-start.14 = (f32[128,1024]{1,0:T(8,128)S(1)}, f32[128,1024]{1,0:T(8,128)S(1)}, u32[]{:S(2)}, u32[]{:S(2)}) collective-permute-start(f32[128,1024]{1,0:T(8,128)S(1)} %get-tuple-element.32), channel_id=1, source_target_pairs={{7,0},{8,1},{9,2},{10,3},{11,4},{12,5},{13,6},{14,7},{15,8},{16,9}... | collective-permute-start | bytes 1572872 | tf_op jit(solution)/shard_map/ppermute | solution.py:16
  240.9 4.8 %copy-start.12 = (u32[256]{0:T(256)S(1)}, u32[256]{0:T(256)}, u32[]{:S(2)}) copy-start(u32[256]{0:T(256)} %constant.41) | copy-start | bytes 3076
  242.2 29.1 %all-to-all-start = ((bf16[8,128,4,8,1,20]{1,3,5,4,2,0:T(8,128)(2,1)}), bf16[8,128,4,8,1,20]{1,3,5,4,2,0:T(8,128)(2,1)S(1)}, u32[]{:S(2)}, u32[]{:S(2)}) async-start(bf16[8,128,4,8,1,20]{1,3,5,4,2,0:T(8,128)(2,1)} %copy.113), calls=%async_computation | async-start | bytes 2621440 | tf_op jit(solution)/shard_map/all_to_all | solution.py:37
  304.4 89.5 %copy-start.5 = (bf16[1152,512]{0,1:T(8,128)(2,1)S(1)}, bf16[1152,512]{0,1:T(8,128)(2,1)}, u32[]{:S(2)}) copy-start(bf16[1152,512]{0,1:T(8,128)(2,1)} %copy-done.4) | copy-start | bytes 3538948
  392.5 6.4 %copy-start.6 = (bf16[4,128,5,128]{3,1,2,0:T(8,128)(2,1)S(1)}, bf16[4,128,5,128]{3,1,2,0:T(8,128)(2,1)}, u32[]{:S(2)}) copy-start(bf16[4,128,5,128]{3,1,2,0:T(8,128)(2,1)} %get-tuple-element.40) | copy-start | bytes 1966084
  392.5 22.9 %collective-permute-start.21 = (f32[4,1024]{1,0:T(4,128)S(1)}, f32[4,1024]{1,0:T(4,128)S(1)}, u32[]{:S(2)}, u32[]{:S(2)}) collective-permute-start(f32[4,1024]{1,0:T(4,128)S(1)} %slice.72), channel_id=1, source_target_pairs={{0,48},{8,56},{16,64},{24,72},{32,80},{40,88},{48,96},{56,104},{64... | collective-permute-start | bytes 49160
  397.8 21.0 %copy-start.9 = (bf16[128,1024]{1,0:T(8,128)(2,1)S(1)}, bf16[128,1024]{1,0:T(8,128)(2,1)}, u32[]{:S(2)}) copy-start(bf16[128,1024]{1,0:T(8,128)(2,1)} %fusion.32) | copy-start | bytes 786436
  400.0 19.5 %collective-permute-start.20 = (f32[24,1024]{1,0:T(8,128)S(1)}, f32[24,1024]{1,0:T(8,128)S(1)}, u32[]{:S(2)}, u32[]{:S(2)}) collective-permute-start(f32[24,1024]{1,0:T(8,128)S(1)} %fusion), channel_id=1, source_target_pairs={{0,40},{8,48},{16,56},{24,64},{32,72},{40,80},{48,88},{56,96},{64,... | collective-permute-start | bytes 294920
  401.3 18.2 %collective-permute-start.19 = (f32[24,1024]{1,0:T(8,128)S(1)}, f32[24,1024]{1,0:T(8,128)S(1)}, u32[]{:S(2)}, u32[]{:S(2)}) collective-permute-start(f32[24,1024]{1,0:T(8,128)S(1)} %fusion), channel_id=1, source_target_pairs={{0,32},{8,40},{16,48},{24,56},{32,64},{40,72},{48,80},{56,88},{64,... | collective-permute-start | bytes 294920
  406.5 13.1 %collective-permute-start.18 = (f32[24,1024]{1,0:T(8,128)S(1)}, f32[24,1024]{1,0:T(8,128)S(1)}, u32[]{:S(2)}, u32[]{:S(2)}) collective-permute-start(f32[24,1024]{1,0:T(8,128)S(1)} %fusion), channel_id=1, source_target_pairs={{0,24},{8,32},{16,40},{24,48},{32,56},{40,64},{48,72},{56,80},{64,... | collective-permute-start | bytes 294920
  411.6 10.5 %collective-permute-start.17 = (f32[24,1024]{1,0:T(8,128)S(1)}, f32[24,1024]{1,0:T(8,128)S(1)}, u32[]{:S(2)}, u32[]{:S(2)}) collective-permute-start(f32[24,1024]{1,0:T(8,128)S(1)} %fusion), channel_id=1, source_target_pairs={{0,16},{8,24},{16,32},{24,40},{32,48},{40,56},{48,64},{56,72},{64,... | collective-permute-start | bytes 294920
  415.4 8.0 %collective-permute-start.16 = (f32[24,1024]{1,0:T(8,128)S(1)}, f32[24,1024]{1,0:T(8,128)S(1)}, u32[]{:S(2)}, u32[]{:S(2)}) collective-permute-start(f32[24,1024]{1,0:T(8,128)S(1)} %fusion), channel_id=1, source_target_pairs={{0,8},{8,16},{16,24},{24,32},{32,40},{40,48},{48,56},{56,64},{64,7... | collective-permute-start | bytes 294920
Sparse Core Ops, SparseCore 0:
  238.6 61.0 all-gather.1
